TPU v7x, 128 devices: a whole 4x4x4 slice. The times are simulated.
128 devices in a mesh: leaf: 32 (over x, z, core), level: 4 (over y).
Axes of the slice: x: 4, y: 4, z: 4, core: 2. Of those that a mesh axis runs over, the one named last changes fastest.
Arguments:
- right_side: float32 [8, 2097152], P(None, ('leaf', 'level')), may hold values from -28 to 28
- basis: bfloat16 [16384, 128, 128], P(('leaf', 'level')), may hold values from -0.5 to 0.5
- transfer: bfloat16 [16384, 128, 128], P(('leaf', 'level')), may hold values from -0.5 to 0.5
- order: int32 [128, 128], P(('leaf', 'level')), may hold values from 0 to 127, each once within a row
- far_src: int32 [4096, 4], P(('leaf', 'level')), may hold values from 0 to 127
- far_mats: bfloat16 [4096, 4, 128, 128], P(('leaf', 'level')), may hold values from -0.125 to 0.125
- near_target: int32 [32768], P(('leaf', 'level')), may hold values from 0 to 127
- near_dest: int32 [32768, 1], P(('leaf', 'level')), may hold values from 0 to 127; in each aligned block of 256 rows (0 to 255, 256 to 511, ...) at most 4 rows name the same one
- near_src: int32 [32768], P(('leaf', 'level')), may hold values from 0 to 127
- near_blocks: bfloat16 [32768, 128, 128], P(('leaf', 'level')), may hold values from -0.5 to 0.5
Outputs:
- solution: float32 [8, 2097152], P(None, ('leaf', 'level'))
- residual: float32 [8, 2097152], P(None, ('leaf', 'level'))
Inputs may be any that keep to these rules, and one draw needn't show every extreme that they name: `order`: each group's row is a permutation of 0 to 127. `near_dest`: among the pairs of one group, no group is named more than 4 times, a bound that some block reaches.
All inputs are finite; a program needn't handle non-finite values.
Results may differ from a plain program's by a relative error of at most 0.0022.
Values may be sent and summed in bfloat16 or wider, within the bound.
A program may use at most 128 MiB of HBM per device.

v0:
```python
import jax
import jax.numpy as jnp
from jax import lax
from jax.sharding import PartitionSpec as P

CHILDREN = 4
EPSILON = 1e-06
SCALE = 2.0 ** (-20)


def local(
    right_side,
    basis,
    transfer,
    order,
    far_src,
    far_mats,
    near_target,
    near_dest,
    near_src,
    near_blocks,
):
    systems = right_side.shape[0]
    clusters, points, coeffs = basis.shape
    groups = lax.axis_size(("leaf", "level"))
    capacity = max(4, 2 * near_dest.shape[0] // groups)
    parents = clusters // CHILDREN
    partners = far_src.shape[1]
    permutation = order[0]
    positions = jnp.arange(clusters, dtype=jnp.int32)
    inverse = jnp.zeros((clusters,), jnp.int32).at[permutation].set(positions)
    basis_slot = jnp.take(basis, permutation, axis=0)
    transfer_slot = jnp.take(transfer, permutation, axis=0)
    targets = near_dest[:, 0]
    member = (targets[:, None] == jnp.arange(groups, dtype=jnp.int32)[None, :]).astype(jnp.int32)
    slot_rank = jnp.sum(jnp.cumsum(member, axis=0) * member, axis=1) - 1
    slot_index = targets * capacity + slot_rank
    source_label = (
        jnp.full((groups * capacity,), -1.0, jnp.float32)
        .at[slot_index]
        .set(near_src.astype(jnp.float32))
    )
    cluster_ids = positions.astype(jnp.float32)

    def near_field(rounded):
        columns = jnp.take(rounded, near_target, axis=1)
        partial_rows = jnp.einsum(
            "rnp,npq->nrq", columns, near_blocks, preferred_element_type=jnp.float32
        )
        outgoing = (
            jnp.zeros((groups * capacity, systems, points), jnp.float32)
            .at[slot_index]
            .set(partial_rows)
        )
        incoming, labels = (
            lax.all_to_all(
                outgoing.astype(jnp.bfloat16),
                ("leaf", "level"),
                split_axis=0,
                concat_axis=0,
                tiled=True,
            ).astype(outgoing.dtype),
            lax.all_to_all(
                source_label.astype(jnp.bfloat16),
                ("leaf", "level"),
                split_axis=0,
                concat_axis=0,
                tiled=True,
            ).astype(source_label.dtype),
        )
        landing = (labels[:, None] == cluster_ids[None, :]).astype(jnp.float32)
        return jnp.einsum("sc,srp->rcp", landing, incoming, precision=lax.Precision.HIGHEST)

    def upward(lifted):
        arrived = lax.all_to_all(lifted, ("leaf", "level"), split_axis=0, concat_axis=0, tiled=True)
        return arrived

    def downward(spread):
        returned = lax.all_to_all(
            spread, ("leaf", "level"), split_axis=0, concat_axis=0, tiled=True
        )
        return returned

    def operator(vector_in):
        rounded = vector_in.astype(jnp.bfloat16).reshape(systems, clusters, points)
        near_sum = near_field(rounded)
        ordered = jnp.take(rounded, permutation, axis=1)
        expansion = jnp.einsum(
            "rsp,spk->srk", ordered, basis_slot, preferred_element_type=jnp.float32
        ).astype(jnp.bfloat16)
        lifted = jnp.einsum(
            "srk,skj->srj", expansion, transfer_slot, preferred_element_type=jnp.float32
        )
        arrived = upward(lifted)
        parent_rows = jnp.sum(arrived.reshape(parents, CHILDREN, systems, coeffs), axis=1).astype(
            jnp.bfloat16
        )
        parent_table = lax.all_gather(parent_rows, "level", axis=0, tiled=True)
        picked = jnp.take(parent_table, far_src.reshape(-1), axis=0).reshape(
            parents, partners, systems, coeffs
        )
        translated = jnp.einsum(
            "qfrk,qfkj->qrj", picked, far_mats, preferred_element_type=jnp.float32
        ).astype(jnp.bfloat16)
        returned = downward(jnp.repeat(translated, CHILDREN, axis=0))
        expanded = jnp.einsum(
            "srk,sjk->srj", returned, transfer_slot, preferred_element_type=jnp.float32
        ).astype(jnp.bfloat16)
        far_slot = jnp.einsum(
            "srk,spk->rsp", expanded, basis_slot, preferred_element_type=jnp.float32
        )
        far_sum = jnp.take(far_slot, inverse, axis=1)
        return near_sum + far_sum

    tiles = right_side.reshape(systems, clusters, points)
    image = operator(tiles)
    scaled = image * SCALE
    second = operator(scaled)
    own = jnp.stack(
        [
            jnp.sum(left * right, axis=(1, 2))
            for left, right in (
                (tiles, tiles),
                (tiles, image),
                (image, image),
                (tiles, second),
                (scaled, second),
                (second, second),
            )
        ]
    )
    dots = jnp.sum(lax.all_gather(own, ("leaf", "level")), axis=0)
    first_x, first_z, second_x, second_z, second_u = combine(dots)
    solved = first_x[:, None, None] * tiles + first_z[:, None, None] * image
    left_over = (
        second_x[:, None, None] * tiles
        + second_z[:, None, None] * image
        + second_u[:, None, None] * second
    )
    return (solved.reshape(systems, -1), left_over.reshape(systems, -1))


def combine(dots):
    start_sq = dots[0] + EPSILON
    start_norm = jnp.sqrt(start_sq)
    xx, xz, zz, xu, zu, uu = (dots[k] / start_sq for k in range(6))
    along_one = 0.5 * xx + xz
    kappa = along_one - 0.5
    rest_raw = zz - 2.0 * kappa * xz + kappa * kappa * xx
    rest_sq = rest_raw + EPSILON
    rest_one = jnp.sqrt(rest_sq)
    scaled_rest = SCALE * rest_one
    scaled_sq = scaled_rest * scaled_rest
    xzs = SCALE * xz
    zzs = SCALE * SCALE * zz
    beta = (xz - kappa * xx) / rest_one
    gamma = rest_raw / rest_sq
    one_t = (xu - kappa * xzs) / scaled_rest
    two_t = (zu - kappa * zzs - SCALE * kappa * (xu - kappa * xzs)) / scaled_sq
    t_t = (uu - 2.0 * kappa * zu + kappa * kappa * zzs) / scaled_sq
    cross_two = 0.5 * beta + one_t
    along_two = 0.5 * gamma + two_t
    short = 0.5 - along_two
    tail_sq = (
        t_t
        + short * short * gamma
        + cross_two * cross_two * xx
        + 2.0 * short * two_t
        - 2.0 * cross_two * one_t
        - 2.0 * cross_two * short * beta
    )
    gram_first = along_one * along_one + rest_one * rest_one
    gram_cross = along_one * cross_two + rest_one * along_two
    gram_last = cross_two * cross_two + along_two * along_two + tail_sq
    determinant = gram_first * gram_last - gram_cross * gram_cross
    coef_one = start_norm * (along_one * gram_last - cross_two * gram_cross) / determinant
    coef_two = start_norm * (gram_first * cross_two - gram_cross * along_one) / determinant
    one = coef_one / start_norm
    two = coef_two / (start_norm * rest_one)
    return (
        one - kappa * two,
        two,
        1.0 - 0.5 * one + 0.5 * kappa * two,
        -one - (0.5 - kappa) * two,
        -coef_two / (start_norm * scaled_rest),
    )


def solution(mesh):
    placed = (
        P(None, ("leaf", "level")),
        P(("leaf", "level"), None, None),
        P(("leaf", "level"), None, None),
        P(("leaf", "level"), None),
        P(("leaf", "level"), None),
        P(("leaf", "level"), None, None, None),
        P(("leaf", "level")),
        P(("leaf", "level"), None),
        P(("leaf", "level")),
        P(("leaf", "level"), None, None),
    )
    return jax.shard_map(
        local,
        mesh=mesh,
        in_specs=placed,
        out_specs=(P(None, ("leaf", "level")), P(None, ("leaf", "level"))),
        check_vma=False,
    )
```

profile of v0, /device:TPU:1, one launch (start us, length us, event | category | flops | bytes accessed | tf_op | source)
XLA Modules:
  0.0 271.7 jit_solution(17496570078938637699)
XLA Ops:
  3.9 5.2 %gather_fusion.3 = bf16[128,128,128]{2,1,0:T(8,128)(2,1)} fusion(bf16[128,128,128]{2,1,0:T(8,128)(2,1)} %param.22, s32[1024]{0:T(1024)S(1)} %pad_clamp_fusion.2), kind=kCustom, calls=%fused_computation.6.clone | custom fusion | bytes 8389120 | tf_op jit(solution)/shard_map/jit(_take)/gather | solution.py:33
  9.2 5.2 %gather_fusion.1 = bf16[128,128,128]{2,1,0:T(8,128)(2,1)} fusion(bf16[128,128,128]{2,1,0:T(8,128)(2,1)} %param.21, s32[1024]{0:T(1024)S(1)} %pad_clamp_fusion.2), kind=kCustom, calls=%fused_computation.1.clone | custom fusion | bytes 8389120 | tf_op jit(solution)/shard_map/jit(_take)/gather | solution.py:32
  14.4 6.7 %fusion.2 = f32[128,8,128]{2,1,0:T(8,128)} fusion(bf16[128,8,128]{2,1,0:T(8,128)(2,1)S(1)} %gather_fusion.2, pred[128]{0:T(512)(128)(4,1)S(1)} %compare_and_fusion.2, bf16[128,128,128]{2,1,0:T(8,128)(2,1)} %gather_fusion.1, bf16[128,128,128]{2,1,0:T(8,128)(2,1)} %gather_fusion.3), kind=kOutput, calls=%fused_computation.26 | convolution fusion | flops 71565312 | bytes 9175168 | tf_op jit(solution)/shard_map/srk,skj->srj/dot_general | solution.py:91
  21.1 12.0 %all-to-all-start.2 = ((f32[128,8,128]{2,1,0:T(8,128)}), f32[128,8,128]{2,1,0:T(8,128)}, u32[]{:S(2)}, u32[]{:S(2)}) async-start(f32[128,8,128]{2,1,0:T(8,128)} %fusion.2), calls=%async_computation.2 | async-start | bytes 1048576 | tf_op jit(solution)/shard_map/all_to_all | solution.py:75
  36.9 4.7 %fusion.10 = f32[256,8,128]{2,1,0:T(8,128)S(1)} fusion(bf16[256,128,128]{2,1,0:T(8,128)(2,1)} %param.29, bf16[256,8,128]{2,1,0:T(8,128)(2,1)S(1)} %gather_fusion, pred[256]{0:T(512)(128)(4,1)S(1)} %compare_and_fusion.3), kind=kOutput, calls=%fused_computation.41 | convolution fusion | flops 67371008 | bytes 9961728 | tf_op jit(solution)/shard_map/rnp,npq->nrq/dot_general | solution.py:47
  41.8 7.0 %scatter_fusion = f32[512,8,128]{2,1,0:T(8,128)S(1)} fusion(f32[512,8,128]{2,1,0:T(8,128)S(1)} %broadcast.333.clone, s32[256]{0:T(256)S(1)} %bitcast.177, f32[256,8,128]{2,1,0:T(8,128)S(1)} %fusion.10), kind=kCustom, calls=%fused_computation.10 | custom fusion | bytes 3146752 | tf_op jit(solution)/shard_map/scatter | solution.py:53
  51.1 9.8 %all-to-all-start.1 = ((bf16[128,4,1]{1,2,0:T(2,128)(2,1)}), bf16[128,4,1]{1,2,0:T(2,128)(2,1)S(1)}, u32[]{:S(2)}, u32[]{:S(2)}) async-start(bf16[128,4,1]{1,2,0:T(2,128)(2,1)} %all_to_all.33), calls=%async_computation.1 | async-start | bytes 131072 | tf_op jit(solution)/shard_map/all_to_all | solution.py:63
  61.9 10.6 %all_gather.12 = bf16[128,8,128]{2,1,0:T(8,128)(2,1)S(1)} all-gather(bf16[32,8,128]{2,1,0:T(8,128)(2,1)S(1)} %bitcast_reduce_fusion.1), channel_id=1, replica_groups=mesh['leaf'=32,'level'=4] {'level'}, dimensions={0}, use_global_device_ids=true | all-gather | bytes 327680 | tf_op jit(solution)/shard_map/all_gather | solution.py:98
  77.0 11.4 %all-to-all-start.3 = ((bf16[128,8,128]{2,1,0:T(8,128)(2,1)}), bf16[128,8,128]{2,1,0:T(8,128)(2,1)S(1)}, u32[]{:S(2)}, u32[]{:S(2)}) async-start(bf16[128,8,128]{2,1,0:T(8,128)(2,1)} %bitcast.20), calls=%async_computation.3 | async-start | bytes 524288 | tf_op jit(solution)/shard_map/all_to_all | solution.py:79
  88.5 11.3 %all-to-all-done.3 = bf16[128,8,128]{2,1,0:T(8,128)(2,1)S(1)} async-done(((bf16[128,8,128]{2,1,0:T(8,128)(2,1)}), bf16[128,8,128]{2,1,0:T(8,128)(2,1)S(1)}, u32[]{:S(2)}, u32[]{:S(2)}) %all-to-all-start.3) | async-done | bytes 262176 | tf_op jit(solution)/shard_map/all_to_all | solution.py:79
  99.8 3.9 %all-to-all-start = ((bf16[512,8,128]{2,1,0:T(8,128)(2,1)}), bf16[512,8,128]{2,1,0:T(8,128)(2,1)S(1)}, u32[]{:S(2)}, u32[]{:S(2)}) async-start(bf16[512,8,128]{2,1,0:T(8,128)(2,1)} %convert_element_type.72), calls=%async_computation | async-start | bytes 2097152 | tf_op jit(solution)/shard_map/all_to_all | solution.py:56
  104.0 6.9 %convolution_bitcast_fusion.1 = f32[8,128,128]{2,0,1:T(8,128)S(1)} fusion(bf16[128,8,128]{2,1,0:T(8,128)(2,1)S(1)} %all-to-all-done.3, bf16[128,128,128]{2,1,0:T(8,128)(2,1)} %gather_fusion.1, pred[128]{0:T(512)(128)(4,1)S(1)} %compare_and_fusion.2, bf16[128,128,128]{2,1,0:T(8,128)(2,1)} %gather_fusion.3), kind=kOutput, calls=%fused_computation.17 | convolution fusion | flops 71434240 | bytes 9175168 | tf_op jit(solution)/shard_map/srk,spk->rsp/dot_general | solution.py:109
  111.9 11.5 %all-to-all-done = bf16[512,8,128]{2,1,0:T(8,128)(2,1)S(1)} async-done(((bf16[512,8,128]{2,1,0:T(8,128)(2,1)}), bf16[512,8,128]{2,1,0:T(8,128)(2,1)S(1)}, u32[]{:S(2)}, u32[]{:S(2)}) %all-to-all-start) | async-done | bytes 1048608 | tf_op jit(solution)/shard_map/all_to_all | solution.py:56
  125.6 6.6 %fusion.3 = f32[128,8,128]{2,1,0:T(8,128)} fusion(bf16[128,8,128]{2,1,0:T(8,128)(2,1)S(1)} %gather_fusion.7, pred[128]{0:T(512)(128)(4,1)S(1)} %compare_and_fusion.2, bf16[128,128,128]{2,1,0:T(8,128)(2,1)} %gather_fusion.1, bf16[128,128,128]{2,1,0:T(8,128)(2,1)} %gather_fusion.3), kind=kOutput, calls=%fused_computation.27 | convolution fusion | flops 71565312 | bytes 9175168 | tf_op jit(solution)/shard_map/srk,skj->srj/dot_general | solution.py:91
  132.2 3.7 %all-to-all-start.5 = ((f32[128,8,128]{2,1,0:T(8,128)}), f32[128,8,128]{2,1,0:T(8,128)S(1)}, u32[]{:S(2)}, u32[]{:S(2)}) async-start(f32[128,8,128]{2,1,0:T(8,128)} %fusion.3), calls=%async_computation.5 | async-start | bytes 1048576 | tf_op jit(solution)/shard_map/all_to_all | solution.py:75
  136.7 13.5 %all-to-all-done.5 = f32[128,8,128]{2,1,0:T(8,128)S(1)} async-done(((f32[128,8,128]{2,1,0:T(8,128)}), f32[128,8,128]{2,1,0:T(8,128)S(1)}, u32[]{:S(2)}, u32[]{:S(2)}) %all-to-all-start.5) | async-done | bytes 524320 | tf_op jit(solution)/shard_map/all_to_all | solution.py:75
  150.2 9.4 %all_gather.13 = bf16[128,8,128]{2,1,0:T(8,128)(2,1)S(1)} all-gather(bf16[32,8,128]{2,1,0:T(8,128)(2,1)S(1)} %bitcast_reduce_fusion), channel_id=1, replica_groups=mesh['leaf'=32,'level'=4] {'level'}, dimensions={0}, use_global_device_ids=true | all-gather | bytes 327680 | tf_op jit(solution)/shard_map/all_gather | solution.py:98
  164.1 7.6 %all-to-all-start.6 = ((bf16[128,8,128]{2,1,0:T(8,128)(2,1)}), bf16[128,8,128]{2,1,0:T(8,128)(2,1)S(1)}, u32[]{:S(2)}, u32[]{:S(2)}) async-start(bf16[128,8,128]{2,1,0:T(8,128)(2,1)} %bitcast.32), calls=%async_computation.6 | async-start | bytes 524288 | tf_op jit(solution)/shard_map/all_to_all | solution.py:79
  171.7 4.7 %fusion.8 = f32[256,8,128]{2,1,0:T(8,128)S(1)} fusion(bf16[256,128,128]{2,1,0:T(8,128)(2,1)} %param.29, bf16[256,8,128]{2,1,0:T(8,128)(2,1)S(1)} %gather_fusion.6, pred[256]{0:T(512)(128)(4,1)S(1)} %compare_and_fusion.3), kind=kOutput, calls=%fused_computation.38 | convolution fusion | flops 67371008 | bytes 9961728 | tf_op jit(solution)/shard_map/rnp,npq->nrq/dot_general | solution.py:47
  176.6 7.0 %scatter_fusion.1 = f32[512,8,128]{2,1,0:T(8,128)S(1)} fusion(f32[512,8,128]{2,1,0:T(8,128)S(1)} %broadcast.333, s32[256]{0:T(256)S(1)} %bitcast.178, f32[256,8,128]{2,1,0:T(8,128)S(1)} %fusion.8), kind=kCustom, calls=%fused_computation.13 | custom fusion | bytes 3146752 | tf_op jit(solution)/shard_map/scatter | solution.py:53
  184.7 10.2 %all-to-all-start.4 = ((bf16[512,8,128]{2,1,0:T(8,128)(2,1)}), bf16[512,8,128]{2,1,0:T(8,128)(2,1)}, u32[]{:S(2)}, u32[]{:S(2)}) async-start(bf16[512,8,128]{2,1,0:T(8,128)(2,1)} %convert_element_type.83), calls=%async_computation.4 | async-start | bytes 2097152 | tf_op jit(solution)/shard_map/all_to_all | solution.py:56
  195.3 7.0 %convolution_bitcast_fusion = f32[8,128,128]{2,0,1:T(8,128)S(1)} fusion(bf16[128,8,128]{2,1,0:T(8,128)(2,1)S(1)} %all-to-all-done.6, bf16[128,128,128]{2,1,0:T(8,128)(2,1)} %gather_fusion.1, pred[128]{0:T(512)(128)(4,1)S(1)} %compare_and_fusion.2, bf16[128,128,128]{2,1,0:T(8,128)(2,1)} %gather_fusion.3), kind=kOutput, calls=%fused_computation.16 | convolution fusion | flops 71434240 | bytes 9175168 | tf_op jit(solution)/shard_map/srk,spk->rsp/dot_general | solution.py:109
  203.3 11.0 %all-to-all-done.4 = bf16[512,8,128]{2,1,0:T(8,128)(2,1)} async-done(((bf16[512,8,128]{2,1,0:T(8,128)(2,1)}), bf16[512,8,128]{2,1,0:T(8,128)(2,1)}, u32[]{:S(2)}, u32[]{:S(2)}) %all-to-all-start.4) | async-done | bytes 1048608 | tf_op jit(solution)/shard_map/all_to_all | solution.py:56
  216.3 53.0 %all-gather.1 = f32[128,6,8]{2,1,0:T(8,128)S(1)} all-gather(f32[1,6,8]{2,1,0:T(8,128)S(1)} %bitcast.172), channel_id=2, replica_groups=mesh['leaf'=32,'level'=4] {'leaf','level'}, dimensions={0}, use_global_device_ids=true | all-gather | bytes 24768 | tf_op jit(solution)/shard_map/all_gather | solution.py:132
  (89 shorter events, 30.8 us)
Async XLA Ops:
  14.4 18.6 %copy-start.6 = (s32[1,128]{1,0:T(1,128)S(1)}, s32[1,128]{1,0:T(1,128)}, u32[]{:S(2)}) copy-start(s32[1,128]{1,0:T(1,128)} %param.23) | copy-start | bytes 1540
  14.4 18.7 %copy-start.4 = (s32[256]{0:T(256)S(1)}, s32[256]{0:T(256)}, u32[]{:S(2)}) copy-start(s32[256]{0:T(256)} %param.26) | copy-start | bytes 3076
  14.4 18.7 %copy-start.5 = (s32[256]{0:T(256)S(1)}, s32[256]{0:T(256)}, u32[]{:S(2)}) copy-start(s32[256]{0:T(256)} %param.28) | copy-start | bytes 3076
  14.4 18.7 %copy-start.3 = (s32[32,4]{0,1:T(4,128)S(1)}, s32[32,4]{0,1:T(4,128)}, u32[]{:S(2)}) copy-start(s32[32,4]{0,1:T(4,128)} %param.24) | copy-start | bytes 1540
  14.4 18.9 %copy-start.2 = (s32[256,1]{0,1:T(1,128)S(1)}, s32[256,1]{0,1:T(1,128)}, u32[]{:S(2)}) copy-start(s32[256,1]{0,1:T(1,128)} %param.27) | copy-start | bytes 3076
  21.1 30.0 %all-to-all-start.2 = ((f32[128,8,128]{2,1,0:T(8,128)}), f32[128,8,128]{2,1,0:T(8,128)}, u32[]{:S(2)}, u32[]{:S(2)}) async-start(f32[128,8,128]{2,1,0:T(8,128)} %fusion.2), calls=%async_computation.2 | async-start | bytes 1048576 | tf_op jit(solution)/shard_map/all_to_all | solution.py:75
  51.1 25.2 %all-to-all-start.1 = ((bf16[128,4,1]{1,2,0:T(2,128)(2,1)}), bf16[128,4,1]{1,2,0:T(2,128)(2,1)S(1)}, u32[]{:S(2)}, u32[]{:S(2)}) async-start(bf16[128,4,1]{1,2,0:T(2,128)(2,1)} %all_to_all.33), calls=%async_computation.1 | async-start | bytes 131072 | tf_op jit(solution)/shard_map/all_to_all | solution.py:63
  77.0 22.7 %all-to-all-start.3 = ((bf16[128,8,128]{2,1,0:T(8,128)(2,1)}), bf16[128,8,128]{2,1,0:T(8,128)(2,1)S(1)}, u32[]{:S(2)}, u32[]{:S(2)}) async-start(bf16[128,8,128]{2,1,0:T(8,128)(2,1)} %bitcast.20), calls=%async_computation.3 | async-start | bytes 524288 | tf_op jit(solution)/shard_map/all_to_all | solution.py:79
  99.8 23.6 %all-to-all-start = ((bf16[512,8,128]{2,1,0:T(8,128)(2,1)}), bf16[512,8,128]{2,1,0:T(8,128)(2,1)S(1)}, u32[]{:S(2)}, u32[]{:S(2)}) async-start(bf16[512,8,128]{2,1,0:T(8,128)(2,1)} %convert_element_type.72), calls=%async_computation | async-start | bytes 2097152 | tf_op jit(solution)/shard_map/all_to_all | solution.py:56
  132.2 17.9 %all-to-all-start.5 = ((f32[128,8,128]{2,1,0:T(8,128)}), f32[128,8,128]{2,1,0:T(8,128)S(1)}, u32[]{:S(2)}, u32[]{:S(2)}) async-start(f32[128,8,128]{2,1,0:T(8,128)} %fusion.3), calls=%async_computation.5 | async-start | bytes 1048576 | tf_op jit(solution)/shard_map/all_to_all | solution.py:75
  164.1 20.6 %all-to-all-start.6 = ((bf16[128,8,128]{2,1,0:T(8,128)(2,1)}), bf16[128,8,128]{2,1,0:T(8,128)(2,1)S(1)}, u32[]{:S(2)}, u32[]{:S(2)}) async-start(bf16[128,8,128]{2,1,0:T(8,128)(2,1)} %bitcast.32), calls=%async_computation.6 | async-start | bytes 524288 | tf_op jit(solution)/shard_map/all_to_all | solution.py:79
  183.6 11.3 %copy-start.1 = (f32[8,16384]{1,0:T(8,128)S(1)}, f32[8,16384]{1,0:T(8,128)}, u32[]{:S(2)}) copy-start(f32[8,16384]{1,0:T(8,128)} %param.20) | copy-start | bytes 1572868
  184.7 29.6 %all-to-all-start.4 = ((bf16[512,8,128]{2,1,0:T(8,128)(2,1)}), bf16[512,8,128]{2,1,0:T(8,128)(2,1)}, u32[]{:S(2)}, u32[]{:S(2)}) async-start(bf16[512,8,128]{2,1,0:T(8,128)(2,1)} %convert_element_type.83), calls=%async_computation.4 | async-start | bytes 2097152 | tf_op jit(solution)/shard_map/all_to_all | solution.py:56
  195.3 19.1 %copy-start = (f32[8,128,128]{1,2,0:T(8,128)S(1)}, f32[8,128,128]{1,2,0:T(8,128)}, u32[]{:S(2)}) copy-start(f32[8,128,128]{1,2,0:T(8,128)} %get-tuple-element.34) | copy-start | bytes 1572868
where the time goes:
time: 273 us; the launch traced here: 272 us
  blocking collectives  73 us (27%)
  starting transfers between devices  58.5 us (21%)
  waiting for transfers between devices  47.3 us (17%)
  matrix products  45.6 us (17%)
  local copies, waits for them, and re-layouts  38.8 us (14%)
  other arithmetic  7.56 us (3%)
    all_gather x1, blocking collectives, local(): dots = jnp.sum(lax.all_gather(own, ('leaf', 'level')), axis=0)  53 us
    all_to_all x2, waiting for transfers between devices, near_field(): lax.all_to_all(outgoing.astype(jnp.bfloat16), ('leaf', 'level'), split_ax...  22.5 us
    all_gather x2, blocking collectives, operator(): parent_table = lax.all_gather(parent_rows, 'level', axis=0, tiled=True)  20 us
    all_to_all x2, starting transfers between devices, downward(): lax.all_to_all(spread, ('leaf', 'level'), split_axis=0, concat_axis=0, ti...  19 us
    all_to_all x2, starting transfers between devices, upward(): lax.all_to_all(lifted, ('leaf', 'level'), split_axis=0, concat_axis=0, ti...  15.6 us
    all_to_all x2, starting transfers between devices, near_field(): lax.all_to_all(outgoing.astype(jnp.bfloat16), ('leaf', 'level'), split_ax...  14.1 us
    scatter x2, local copies, waits for them, and re-layouts, near_field(): outgoing = jnp.zeros((groups * capacity, systems, points), jnp.float32).a...  14.1 us
    dot_general x2, matrix products, operator(): jnp.einsum('srk,spk->rsp', expanded, basis_slot, preferred_element_type=j...  13.9 us
  transfers between devices with their start and end apart: 7, of which 4 were waited for; matrix products, arithmetic and copies ran while one was open for 19% of the time, Pallas kernels for 0%

commit v1 on v0

--- a/solution.py
+++ b/solution.py
@@ -95,7 +95,9 @@
         parent_rows = jnp.sum(arrived.reshape(parents, CHILDREN, systems, coeffs), axis=1).astype(
             jnp.bfloat16
         )
-        parent_table = lax.all_gather(parent_rows, "level", axis=0, tiled=True)
+        parent_table = jnp.concatenate(
+            lax.all_to_all(jnp.stack([parent_rows] * lax.axis_size("level")), "level", 0, 0), axis=0
+        )
         picked = jnp.take(parent_table, far_src.reshape(-1), axis=0).reshape(
             parents, partners, systems, coeffs
         )

time: 273 us -> 267 us (0.978)
  starting transfers between devices: 58.5 us -> 51.4 us
  waiting for transfers between devices: 47.3 us -> 51.4 us
    all_gather x2 -> x0, blocking collectives: 20 us -> none  [operator(): parent_table = lax.all_gather(parent_rows, 'level', axis=0, tiled=True)]
    all_to_all x0 -> x1, blocking collectives: none -> 17.4 us  [upward(): lax.all_to_all(lifted, ('leaf', 'level'), split_axis=0, concat_axis=0, ti...]
    all_to_all x2 -> x1, waiting for transfers between devices: 13.5 us -> 0.01 us  [upward(): lax.all_to_all(lifted, ('leaf', 'level'), split_axis=0, concat_axis=0, ti...]
    all_to_all x0 -> x2, waiting for transfers between devices: none -> 11.5 us  [operator(): lax.all_to_all(jnp.stack([parent_rows] * lax.axis_size('level')), 'level'...]
    all_to_all x2, starting transfers between devices: 19 us -> 8.43 us  [downward(): lax.all_to_all(spread, ('leaf', 'level'), split_axis=0, concat_axis=0, ti...]
    all_to_all x0 -> x2, starting transfers between devices: none -> 7.57 us  [operator(): lax.all_to_all(jnp.stack([parent_rows] * lax.axis_size('level')), 'level'...]
    all_to_all x1, waiting for transfers between devices: 0.01 us -> 6.07 us  [near_field(): lax.all_to_all(source_label.astype(jnp.bfloat16), ('leaf', 'level'), spli...]
    all_to_all x2 -> x1, starting transfers between devices: 15.6 us -> 12 us  [upward(): lax.all_to_all(lifted, ('leaf', 'level'), split_axis=0, concat_axis=0, ti...]
  transfers between devices with their start and end apart: 7 -> 8, of which waited for: 4 -> 6; matrix products, arithmetic and copies ran while one was open for 19% -> 19% of each run, Pallas kernels for 0% -> 0%
where the time goes in v1:
time: 267 us; the launch traced here: 266 us
  blocking collectives  70.3 us (26%)
  starting transfers between devices  51.4 us (19%)
  waiting for transfers between devices  51.4 us (19%)
  matrix products  43.8 us (16%)
  local copies, waits for them, and re-layouts  40.2 us (15%)
  other arithmetic  7.55 us (3%)
    all_gather x1, blocking collectives, local(): dots = jnp.sum(lax.all_gather(own, ('leaf', 'level')), axis=0)  53 us
    all_to_all x2, waiting for transfers between devices, near_field(): lax.all_to_all(outgoing.astype(jnp.bfloat16), ('leaf', 'level'), split_ax...  22.5 us
    all_to_all x1, blocking collectives, upward(): lax.all_to_all(lifted, ('leaf', 'level'), split_axis=0, concat_axis=0, ti...  17.4 us
    all_to_all x2, starting transfers between devices, near_field(): lax.all_to_all(outgoing.astype(jnp.bfloat16), ('leaf', 'level'), split_ax...  14.2 us
    scatter x2, local copies, waits for them, and re-layouts, near_field(): outgoing = jnp.zeros((groups * capacity, systems, points), jnp.float32).a...  14.1 us
    dot_general x2, matrix products, operator(): jnp.einsum('srk,spk->rsp', expanded, basis_slot, preferred_element_type=j...  13.9 us
    all_to_all x1, starting transfers between devices, upward(): lax.all_to_all(lifted, ('leaf', 'level'), split_axis=0, concat_axis=0, ti...  12 us
    all_to_all x2, waiting for transfers between devices, operator(): lax.all_to_all(jnp.stack([parent_rows] * lax.axis_size('level')), 'level'...  11.5 us
  transfers between devices with their start and end apart: 8, of which 6 were waited for; matrix products, arithmetic and copies ran while one was open for 19% of the time, Pallas kernels for 0%

profile of v1, /device:TPU:1, one launch (start us, length us, event | category | flops | bytes accessed | tf_op | source)
XLA Modules:
  0.0 265.8 jit_solution(9308878808702137166)
XLA Ops:
  3.9 5.2 %gather_fusion.3 = bf16[128,128,128]{2,1,0:T(8,128)(2,1)} fusion(bf16[128,128,128]{2,1,0:T(8,128)(2,1)} %param.22, s32[1024]{0:T(1024)S(1)} %pad_clamp_fusion.2), kind=kCustom, calls=%fused_computation.6.clone | custom fusion | bytes 8389120 | tf_op jit(solution)/shard_map/jit(_take)/gather | solution.py:33
  9.2 5.2 %gather_fusion.1 = bf16[128,128,128]{2,1,0:T(8,128)(2,1)} fusion(bf16[128,128,128]{2,1,0:T(8,128)(2,1)} %param.21, s32[1024]{0:T(1024)S(1)} %pad_clamp_fusion.2), kind=kCustom, calls=%fused_computation.1.clone | custom fusion | bytes 8389120 | tf_op jit(solution)/shard_map/jit(_take)/gather | solution.py:32
  14.4 6.7 %fusion.2 = f32[128,8,128]{2,1,0:T(8,128)} fusion(bf16[128,8,128]{2,1,0:T(8,128)(2,1)S(1)} %gather_fusion.2, pred[128]{0:T(512)(128)(4,1)S(1)} %compare_and_fusion.2, bf16[128,128,128]{2,1,0:T(8,128)(2,1)} %gather_fusion.1, bf16[128,128,128]{2,1,0:T(8,128)(2,1)} %gather_fusion.3), kind=kOutput, calls=%fused_computation.26 | convolution fusion | flops 71565312 | bytes 9175168 | tf_op jit(solution)/shard_map/srk,skj->srj/dot_general | solution.py:91
  21.0 12.0 %all-to-all-start.2 = ((f32[128,8,128]{2,1,0:T(8,128)}), f32[128,8,128]{2,1,0:T(8,128)}, u32[]{:S(2)}, u32[]{:S(2)}) async-start(f32[128,8,128]{2,1,0:T(8,128)} %fusion.2), calls=%async_computation.2 | async-start | bytes 1048576 | tf_op jit(solution)/shard_map/all_to_all | solution.py:75
  36.9 4.7 %fusion.10 = f32[256,8,128]{2,1,0:T(8,128)S(1)} fusion(bf16[256,128,128]{2,1,0:T(8,128)(2,1)} %param.29, bf16[256,8,128]{2,1,0:T(8,128)(2,1)S(1)} %gather_fusion, pred[256]{0:T(512)(128)(4,1)S(1)} %compare_and_fusion.3), kind=kOutput, calls=%fused_computation.41 | convolution fusion | flops 67371008 | bytes 9961728 | tf_op jit(solution)/shard_map/rnp,npq->nrq/dot_general | solution.py:47
  41.8 7.0 %scatter_fusion = f32[512,8,128]{2,1,0:T(8,128)S(1)} fusion(f32[512,8,128]{2,1,0:T(8,128)S(1)} %broadcast.335.clone, s32[256]{0:T(256)S(1)} %bitcast.181, f32[256,8,128]{2,1,0:T(8,128)S(1)} %fusion.10), kind=kCustom, calls=%fused_computation.10 | custom fusion | bytes 3146752 | tf_op jit(solution)/shard_map/scatter | solution.py:53
  52.9 4.2 %all-to-all-start.3 = ((bf16[4,32,8,128]{3,2,1,0:T(8,128)(2,1)}), bf16[4,32,8,128]{3,2,1,0:T(8,128)(2,1)S(1)}, u32[]{:S(2)}, u32[]{:S(2)}) async-start(bf16[4,32,8,128]{3,2,1,0:T(8,128)(2,1)} %stack.36), calls=%async_computation.3 | async-start | bytes 524288 | tf_op jit(solution)/shard_map/all_to_all | solution.py:99
  57.0 5.8 %all-to-all-done.3 = bf16[4,32,8,128]{3,2,1,0:T(8,128)(2,1)S(1)} async-done(((bf16[4,32,8,128]{3,2,1,0:T(8,128)(2,1)}), bf16[4,32,8,128]{3,2,1,0:T(8,128)(2,1)S(1)}, u32[]{:S(2)}, u32[]{:S(2)}) %all-to-all-start.3) | async-done | bytes 262176 | tf_op jit(solution)/shard_map/all_to_all | solution.py:99
  62.8 9.2 %all-to-all-start.1 = ((bf16[128,4,1]{1,2,0:T(2,128)(2,1)}), bf16[128,4,1]{1,2,0:T(2,128)(2,1)S(1)}, u32[]{:S(2)}, u32[]{:S(2)}) async-start(bf16[128,4,1]{1,2,0:T(2,128)(2,1)} %all_to_all.41), calls=%async_computation.1 | async-start | bytes 131072 | tf_op jit(solution)/shard_map/all_to_all | solution.py:63
  75.8 6.1 %all-to-all-done.1 = bf16[128,4,1]{1,2,0:T(2,128)(2,1)S(1)} async-done(((bf16[128,4,1]{1,2,0:T(2,128)(2,1)}), bf16[128,4,1]{1,2,0:T(2,128)(2,1)S(1)}, u32[]{:S(2)}, u32[]{:S(2)}) %all-to-all-start.1) | async-done | bytes 1056 | tf_op jit(solution)/shard_map/all_to_all | solution.py:63
  82.6 4.0 %all-to-all-start.4 = ((bf16[128,8,128]{2,1,0:T(8,128)(2,1)}), bf16[128,8,128]{2,1,0:T(8,128)(2,1)S(1)}, u32[]{:S(2)}, u32[]{:S(2)}) async-start(bf16[128,8,128]{2,1,0:T(8,128)(2,1)} %bitcast.21), calls=%async_computation.4 | async-start | bytes 524288 | tf_op jit(solution)/shard_map/all_to_all | solution.py:79
  86.6 11.3 %all-to-all-done.4 = bf16[128,8,128]{2,1,0:T(8,128)(2,1)S(1)} async-done(((bf16[128,8,128]{2,1,0:T(8,128)(2,1)}), bf16[128,8,128]{2,1,0:T(8,128)(2,1)S(1)}, u32[]{:S(2)}, u32[]{:S(2)}) %all-to-all-start.4) | async-done | bytes 262176 | tf_op jit(solution)/shard_map/all_to_all | solution.py:79
  102.1 6.9 %convolution_bitcast_fusion.1 = f32[8,128,128]{2,0,1:T(8,128)S(1)} fusion(bf16[128,8,128]{2,1,0:T(8,128)(2,1)S(1)} %all-to-all-done.4, bf16[128,128,128]{2,1,0:T(8,128)(2,1)} %gather_fusion.1, pred[128]{0:T(512)(128)(4,1)S(1)} %compare_and_fusion.2, bf16[128,128,128]{2,1,0:T(8,128)(2,1)} %gather_fusion.3), kind=kOutput, calls=%fused_computation.17 | convolution fusion | flops 71434240 | bytes 9175168 | tf_op jit(solution)/shard_map/srk,spk->rsp/dot_general | solution.py:111
  110.0 11.5 %all-to-all-done = bf16[512,8,128]{2,1,0:T(8,128)(2,1)S(1)} async-done(((bf16[512,8,128]{2,1,0:T(8,128)(2,1)}), bf16[512,8,128]{2,1,0:T(8,128)(2,1)S(1)}, u32[]{:S(2)}, u32[]{:S(2)}) %all-to-all-start) | async-done | bytes 1048608 | tf_op jit(solution)/shard_map/all_to_all | solution.py:56
  123.8 4.8 %fusion.3 = f32[128,8,128]{2,1,0:T(8,128)S(1)} fusion(bf16[128,8,128]{2,1,0:T(8,128)(2,1)S(1)} %gather_fusion.7, pred[128]{0:T(512)(128)(4,1)S(1)} %compare_and_fusion.2, bf16[128,128,128]{2,1,0:T(8,128)(2,1)} %gather_fusion.1, bf16[128,128,128]{2,1,0:T(8,128)(2,1)} %gather_fusion.3), kind=kOutput, calls=%fused_computation.27 | convolution fusion | flops 71565312 | bytes 9175168 | tf_op jit(solution)/shard_map/srk,skj->srj/dot_general | solution.py:91
  128.5 17.4 %all_to_all.51 = f32[128,8,128]{2,1,0:T(8,128)S(1)} all-to-all(f32[128,8,128]{2,1,0:T(8,128)S(1)} %fusion.3), channel_id=1, replica_groups=mesh['leaf'=32,'level'=4] {'leaf','level'}, dimensions={0} | all-to-all | bytes 1048576 | tf_op jit(solution)/shard_map/all_to_all | solution.py:75
  150.9 5.7 %all-to-all-done.7 = bf16[4,32,8,128]{3,2,1,0:T(8,128)(2,1)S(1)} async-done(((bf16[4,32,8,128]{3,2,1,0:T(8,128)(2,1)}), bf16[4,32,8,128]{3,2,1,0:T(8,128)(2,1)S(1)}, u32[]{:S(2)}, u32[]{:S(2)}) %all-to-all-start.7) | async-done | bytes 262176 | tf_op jit(solution)/shard_map/all_to_all | solution.py:99
  161.1 4.5 %all-to-all-start.8 = ((bf16[128,8,128]{2,1,0:T(8,128)(2,1)}), bf16[128,8,128]{2,1,0:T(8,128)(2,1)S(1)}, u32[]{:S(2)}, u32[]{:S(2)}) async-start(bf16[128,8,128]{2,1,0:T(8,128)(2,1)} %bitcast.34), calls=%async_computation.8 | async-start | bytes 524288 | tf_op jit(solution)/shard_map/all_to_all | solution.py:79
  165.6 4.7 %fusion.8 = f32[256,8,128]{2,1,0:T(8,128)S(1)} fusion(bf16[256,128,128]{2,1,0:T(8,128)(2,1)} %param.29, bf16[256,8,128]{2,1,0:T(8,128)(2,1)S(1)} %gather_fusion.6, pred[256]{0:T(512)(128)(4,1)S(1)} %compare_and_fusion.3), kind=kOutput, calls=%fused_computation.38 | convolution fusion | flops 67371008 | bytes 9961728 | tf_op jit(solution)/shard_map/rnp,npq->nrq/dot_general | solution.py:47
  170.5 7.0 %scatter_fusion.1 = f32[512,8,128]{2,1,0:T(8,128)S(1)} fusion(f32[512,8,128]{2,1,0:T(8,128)S(1)} %broadcast.335, s32[256]{0:T(256)S(1)} %bitcast.182, f32[256,8,128]{2,1,0:T(8,128)S(1)} %fusion.8), kind=kCustom, calls=%fused_computation.13 | custom fusion | bytes 3146752 | tf_op jit(solution)/shard_map/scatter | solution.py:53
  178.6 10.4 %all-to-all-start.5 = ((bf16[512,8,128]{2,1,0:T(8,128)(2,1)}), bf16[512,8,128]{2,1,0:T(8,128)(2,1)}, u32[]{:S(2)}, u32[]{:S(2)}) async-start(bf16[512,8,128]{2,1,0:T(8,128)(2,1)} %convert_element_type.87), calls=%async_computation.5 | async-start | bytes 2097152 | tf_op jit(solution)/shard_map/all_to_all | solution.py:56
  189.3 7.0 %convolution_bitcast_fusion = f32[8,128,128]{2,0,1:T(8,128)S(1)} fusion(bf16[128,8,128]{2,1,0:T(8,128)(2,1)S(1)} %all-to-all-done.8, bf16[128,128,128]{2,1,0:T(8,128)(2,1)} %gather_fusion.1, pred[128]{0:T(512)(128)(4,1)S(1)} %compare_and_fusion.2, bf16[128,128,128]{2,1,0:T(8,128)(2,1)} %gather_fusion.3), kind=kOutput, calls=%fused_computation.16 | convolution fusion | flops 71434240 | bytes 9175168 | tf_op jit(solution)/shard_map/srk,spk->rsp/dot_general | solution.py:111
  197.3 11.0 %all-to-all-done.5 = bf16[512,8,128]{2,1,0:T(8,128)(2,1)} async-done(((bf16[512,8,128]{2,1,0:T(8,128)(2,1)}), bf16[512,8,128]{2,1,0:T(8,128)(2,1)}, u32[]{:S(2)}, u32[]{:S(2)}) %all-to-all-start.5) | async-done | bytes 1048608 | tf_op jit(solution)/shard_map/all_to_all | solution.py:56
  210.3 53.0 %all-gather.1 = f32[128,6,8]{2,1,0:T(8,128)S(1)} all-gather(f32[1,6,8]{2,1,0:T(8,128)S(1)} %bitcast.176), channel_id=2, replica_groups=mesh['leaf'=32,'level'=4] {'leaf','level'}, dimensions={0}, use_global_device_ids=true | all-gather | bytes 24768 | tf_op jit(solution)/shard_map/all_gather | solution.py:134
  (92 shorter events, 39.6 us)
Async XLA Ops:
  14.4 18.6 %copy-start.4 = (s32[256]{0:T(256)S(1)}, s32[256]{0:T(256)}, u32[]{:S(2)}) copy-start(s32[256]{0:T(256)} %param.26) | copy-start | bytes 3076
  14.4 18.7 %copy-start.5 = (s32[256]{0:T(256)S(1)}, s32[256]{0:T(256)}, u32[]{:S(2)}) copy-start(s32[256]{0:T(256)} %param.28) | copy-start | bytes 3076
  14.4 18.7 %copy-start.3 = (s32[32,4]{0,1:T(4,128)S(1)}, s32[32,4]{0,1:T(4,128)}, u32[]{:S(2)}) copy-start(s32[32,4]{0,1:T(4,128)} %param.24) | copy-start | bytes 1540
  14.4 18.9 %copy-start.2 = (s32[256,1]{0,1:T(1,128)S(1)}, s32[256,1]{0,1:T(1,128)}, u32[]{:S(2)}) copy-start(s32[256,1]{0,1:T(1,128)} %param.27) | copy-start | bytes 3076
  21.0 30.0 %all-to-all-start.2 = ((f32[128,8,128]{2,1,0:T(8,128)}), f32[128,8,128]{2,1,0:T(8,128)}, u32[]{:S(2)}, u32[]{:S(2)}) async-start(f32[128,8,128]{2,1,0:T(8,128)} %fusion.2), calls=%async_computation.2 | async-start | bytes 1048576 | tf_op jit(solution)/shard_map/all_to_all | solution.py:75
  41.6 8.4 %copy-start.6 = (s32[1,128]{1,0:T(1,128)S(1)}, s32[1,128]{1,0:T(1,128)}, u32[]{:S(2)}) copy-start(s32[1,128]{1,0:T(1,128)} %param.23) | copy-start | bytes 1540
  52.9 10.0 %all-to-all-start.3 = ((bf16[4,32,8,128]{3,2,1,0:T(8,128)(2,1)}), bf16[4,32,8,128]{3,2,1,0:T(8,128)(2,1)S(1)}, u32[]{:S(2)}, u32[]{:S(2)}) async-start(bf16[4,32,8,128]{3,2,1,0:T(8,128)(2,1)} %stack.36), calls=%async_computation.3 | async-start | bytes 524288 | tf_op jit(solution)/shard_map/all_to_all | solution.py:99
  62.8 19.0 %all-to-all-start.1 = ((bf16[128,4,1]{1,2,0:T(2,128)(2,1)}), bf16[128,4,1]{1,2,0:T(2,128)(2,1)S(1)}, u32[]{:S(2)}, u32[]{:S(2)}) async-start(bf16[128,4,1]{1,2,0:T(2,128)(2,1)} %all_to_all.41), calls=%async_computation.1 | async-start | bytes 131072 | tf_op jit(solution)/shard_map/all_to_all | solution.py:63
  82.6 15.3 %all-to-all-start.4 = ((bf16[128,8,128]{2,1,0:T(8,128)(2,1)}), bf16[128,8,128]{2,1,0:T(8,128)(2,1)S(1)}, u32[]{:S(2)}, u32[]{:S(2)}) async-start(bf16[128,8,128]{2,1,0:T(8,128)(2,1)} %bitcast.21), calls=%async_computation.4 | async-start | bytes 524288 | tf_op jit(solution)/shard_map/all_to_all | solution.py:79
  97.9 23.6 %all-to-all-start = ((bf16[512,8,128]{2,1,0:T(8,128)(2,1)}), bf16[512,8,128]{2,1,0:T(8,128)(2,1)S(1)}, u32[]{:S(2)}, u32[]{:S(2)}) async-start(bf16[512,8,128]{2,1,0:T(8,128)(2,1)} %convert_element_type.76), calls=%async_computation | async-start | bytes 2097152 | tf_op jit(solution)/shard_map/all_to_all | solution.py:56
  146.7 9.9 %all-to-all-start.7 = ((bf16[4,32,8,128]{3,2,1,0:T(8,128)(2,1)}), bf16[4,32,8,128]{3,2,1,0:T(8,128)(2,1)S(1)}, u32[]{:S(2)}, u32[]{:S(2)}) async-start(bf16[4,32,8,128]{3,2,1,0:T(8,128)(2,1)} %stack.39), calls=%async_computation.7 | async-start | bytes 524288 | tf_op jit(solution)/shard_map/all_to_all | solution.py:99
  161.1 17.5 %all-to-all-start.8 = ((bf16[128,8,128]{2,1,0:T(8,128)(2,1)}), bf16[128,8,128]{2,1,0:T(8,128)(2,1)S(1)}, u32[]{:S(2)}, u32[]{:S(2)}) async-start(bf16[128,8,128]{2,1,0:T(8,128)(2,1)} %bitcast.34), calls=%async_computation.8 | async-start | bytes 524288 | tf_op jit(solution)/shard_map/all_to_all | solution.py:79
  177.5 11.5 %copy-start.1 = (f32[8,16384]{1,0:T(8,128)S(1)}, f32[8,16384]{1,0:T(8,128)}, u32[]{:S(2)}) copy-start(f32[8,16384]{1,0:T(8,128)} %param.20) | copy-start | bytes 1572868
  178.6 29.8 %all-to-all-start.5 = ((bf16[512,8,128]{2,1,0:T(8,128)(2,1)}), bf16[512,8,128]{2,1,0:T(8,128)(2,1)}, u32[]{:S(2)}, u32[]{:S(2)}) async-start(bf16[512,8,128]{2,1,0:T(8,128)(2,1)} %convert_element_type.87), calls=%async_computation.5 | async-start | bytes 2097152 | tf_op jit(solution)/shard_map/all_to_all | solution.py:56
  189.3 19.1 %copy-start = (f32[8,128,128]{1,2,0:T(8,128)S(1)}, f32[8,128,128]{1,2,0:T(8,128)}, u32[]{:S(2)}) copy-start(f32[8,128,128]{1,2,0:T(8,128)} %get-tuple-element.34) | copy-start | bytes 1572868
